TPU v7x, 32 devices: a whole 2x2x4 slice. The times are simulated.
32 devices in a mesh: groups: 2 (over y), seq: 4 (over z), mp: 2 (over x), enc: 2 (over core).
Axes of the slice: x: 2, y: 2, z: 4, core: 2. Of those that a mesh axis runs over, the one named last changes fastest.
Arguments:
- tokens: bfloat16 [4096, 4096], P(('groups', 'seq'), ('mp', 'enc')), parts along dimension 0, may hold values from -6 to 6
- nbr_feats: bfloat16 [192, 128, 4096], P(('groups', 'seq'), None, ('mp', 'enc')), parts along dimension 0, may hold values from -6 to 6
- counts: int32 [8], P('groups'), parts along dimension 0, may hold values from 8 to 24, as said below
- slot_target: int32 [192], P(('groups', 'seq')), parts along dimension 0, may hold values from 0 to 63, as said below
- w_query: bfloat16 [4096, 512], P(None, ('mp', 'enc')), may hold values from -32 to 32
- w_keyval: bfloat16 [4096, 512], P(None, ('mp', 'enc')), may hold values from -1 to 1
Outputs:
- attended: bfloat16 [4096, 512], P(('groups', 'seq'), ('mp', 'enc')), parts along dimension 0
There are 2 independent parts, one for each index of `groups`. A program takes and returns all parts, laid end to end along the dimension named above; an argument that names none is the same for every part. Nothing has to cross between parts.
Inputs may be any that keep to these rules, and one draw needn't show every extreme that they name: Each seq index's live slots are its first counts slots; the counts sum to 64. `slot_target`: A live slot holds neighbour o * 16 + l of the spans of seq index o; every neighbour is held by exactly one live slot; the live slots of one seq index hold at most 8 neighbours of any one seq index; dead slots hold arbitrary values of the range.
All inputs are finite; a program needn't handle non-finite values.
Results may differ from a plain program's by a relative error of at most 0.003.
The roundings to bfloat16 on the way count: a program that leaves them out, or rounds other values in their place, can miss the bound.
Values may be sent and summed in bfloat16 or wider, within the bound.
A program may use at most 128 MiB of HBM per device.

v0:
```python
import jax
import jax.numpy as jnp
from jax import lax
from jax.sharding import PartitionSpec as P

D = 4096
SPAN = 64
NBR = 2
RLEN = 128
CH_SEQ = 8
NB_SEQ = 16
ENC_CAP = 24
epsilon = 1e-05


def partner_2(block, axis, stride):
    count = lax.axis_size(axis)
    route = []
    for low in range(count):
        high = low | 1 << stride
        if high != low and high < count:
            route += [(low, high), (high, low)]
    return lax.ppermute(block, axis, route)


def passed_along(block, axis, distance):
    devices = range(lax.axis_size(axis))
    route = [(i - distance, i) for i in devices if i - distance in devices]
    return lax.ppermute(block, axis, route)


def project_fold(weight, piece):
    width = piece.shape[-1]
    flat_rows = piece.reshape(-1, width)
    mine = lax.all_to_all(weight, ("mp", "enc"), split_axis=0, concat_axis=1, tiled=True)
    partial = jnp.dot(flat_rows, mine, preferred_element_type=jnp.float32)
    running = lax.psum_scatter(partial, ("mp", "enc"), scatter_dimension=1, tiled=True)
    widened = flat_rows.astype(jnp.float32)
    squares = lax.psum(jnp.sum(widened * widened, axis=1), ("mp", "enc"))
    return (running, squares)


def normalized(carry, factor):
    running, squares = carry
    scale_rows = lax.rsqrt(squares / D + epsilon) * factor
    return (running * scale_rows[:, None]).astype(jnp.bfloat16)


def routing_plan(slot_target, counts, pair_cap):
    seq_count = counts.shape[0]
    seq_here = lax.axis_index("seq")
    live_count = jnp.sum(jnp.where(jnp.arange(seq_count) == seq_here, counts, 0))
    slot_ids = jnp.arange(ENC_CAP)
    live_slots = slot_ids < live_count
    owner_of = slot_target // NB_SEQ
    position = slot_target % NB_SEQ
    same_owner = (
        (owner_of[:, None] == owner_of[None, :])
        & live_slots[None, :]
        & (slot_ids[None, :] < slot_ids[:, None])
    )
    rank_within = jnp.sum(same_owner.astype(jnp.int32), axis=1)
    target_slot = owner_of * pair_cap + rank_within
    buffer_ids = jnp.arange(seq_count * pair_cap)
    chosen = (buffer_ids[:, None] == target_slot[None, :]) & live_slots[None, :]
    sent_ids = jnp.sum(jnp.where(chosen, position[None, :] + 1, 0), axis=1) - 1
    return (chosen, sent_ids.reshape(seq_count, pair_cap))


def pack_rows(chosen, payload, seq_count, pair_cap):
    packed = jnp.dot(chosen.astype(jnp.bfloat16), payload, preferred_element_type=jnp.float32)
    return packed.astype(jnp.bfloat16).reshape(seq_count, pair_cap, payload.shape[1])


def place_rows(received, received_ids):
    flat_rows = received.reshape(-1, received.shape[-1])
    picker = received_ids.reshape(1, -1) == jnp.arange(NB_SEQ)[:, None]
    placed = jnp.dot(picker.astype(jnp.bfloat16), flat_rows, preferred_element_type=jnp.float32)
    return placed.astype(jnp.bfloat16)


def local(tokens, nbr_feats, counts, slot_target, w_query, w_keyval):
    seq_count = lax.axis_size("seq")
    pair_cap = max(2, 2 * NB_SEQ // seq_count)
    head_size = w_keyval.shape[1]
    chosen, sent_ids = routing_plan(slot_target, counts, pair_cap)
    folded = project_fold(w_keyval, nbr_feats)
    encoded = normalized(folded, 1.0).reshape(ENC_CAP, RLEN * head_size)
    packed = pack_rows(chosen, encoded, seq_count, pair_cap)
    received, received_ids = (
        lax.all_to_all(packed, "seq", split_axis=0, concat_axis=0, tiled=True),
        lax.all_to_all(sent_ids, "seq", split_axis=0, concat_axis=0, tiled=True),
    )
    own_half = place_rows(received, received_ids).reshape(NB_SEQ, RLEN, head_size)
    partner = partner_2(own_half, "enc", 0)
    first_lane = lax.axis_index("enc") == 0
    key_rows = jnp.where(first_lane, own_half, partner).reshape(CH_SEQ, NBR * RLEN, head_size)
    value_rows = jnp.where(first_lane, partner, own_half).reshape(CH_SEQ, NBR * RLEN, head_size)
    prior_keys, prior_values = passed_along((key_rows[-1], value_rows[-1]), "seq", 1)
    context_keys = jnp.concatenate([prior_keys[None], key_rows[:-1]], axis=0)
    context_values = jnp.concatenate([prior_values[None], value_rows[:-1]], axis=0)
    folded_tokens = project_fold(w_query, tokens)
    queries = normalized(folded_tokens, head_size ** (-0.5)).reshape(CH_SEQ, SPAN, head_size)
    scores = jnp.einsum("cqd,ckd->cqk", queries, context_keys, preferred_element_type=jnp.float32)
    weights = jax.nn.softmax(scores, axis=-1).astype(jnp.bfloat16)
    attended = jnp.einsum(
        "cqk,ckd->cqd", weights, context_values, preferred_element_type=jnp.float32
    )
    return attended.astype(jnp.bfloat16).reshape(CH_SEQ * SPAN, head_size)


def solution(mesh):
    placed = (
        P(("groups", "seq"), ("mp", "enc")),
        P(("groups", "seq"), None, ("mp", "enc")),
        P("groups"),
        P(("groups", "seq")),
        P(None, ("mp", "enc")),
        P(None, ("mp", "enc")),
    )
    return jax.shard_map(
        local,
        mesh=mesh,
        in_specs=placed,
        out_specs=P(("groups", "seq"), ("mp", "enc")),
        check_vma=False,
    )
```

profile of v0, /device:TPU:0, one launch (start us, length us, event | category | flops | bytes accessed | tf_op | source)
XLA Modules:
  0.0 157.2 jit_solution(10711013462824801652)
XLA Ops:
  6.5 18.7 %all_to_all.49 = bf16[4,1024,128]{2,1,0:T(8,128)(2,1)S(1)} all-to-all(bf16[4,1024,128]{2,1,0:T(8,128)(2,1)} %bitcast.41), channel_id=1, replica_groups=mesh['groups'=2,'seq'=4,'mp'=2,'enc'=2] {'mp','enc'}, dimensions={0} | all-to-all | bytes 2097152 | tf_op jit(solution)/shard_map/all_to_all | solution.py:35
  25.2 0.5 copy.14
  25.7 8.2 %fusion.33 = f32[3072,512]{1,0:T(8,128)} fusion(bf16[3072,1024]{1,0:T(8,128)(2,1)} %bitcast.35, bf16[1024,512]{0,1:T(8,128)(2,1)S(1)} %bitcast.42), kind=kOutput, calls=%fused_computation.53 | convolution fusion | flops 3221225472 | bytes 13631488 | tf_op jit(solution)/shard_map/dot_general | solution.py:36
  34.0 0.6 copy-done.1
  34.6 0.6 fusion.22
  35.3 0.6 iota_compare_fusion.4
  36.3 0.7 sub.20
  36.9 5.6 %all-to-all-start.1 = ((s32[4,1,8]{2,1,0:T(1,128)}), s32[4,1,8]{2,1,0:T(1,128)S(1)}, u32[]{:S(2)}, u32[]{:S(2)}) async-start(s32[4,1,8]{2,1,0:T(1,128)} %bitcast.4), calls=%async_computation.2 | async-start | bytes 4096 | tf_op jit(solution)/shard_map/all_to_all | solution.py:92
  42.8 5.6 %multiply_reduce_fusion = f32[24,128]{1,0:T(8,128)S(1)} fusion(bf16[24,128,1024]{2,1,0:T(8,128)(2,1)} %param.7), kind=kLoop, calls=%fused_computation.4 | loop fusion | flops 9434112 | bytes 6303744 | tf_op jit(solution)/shard_map/reduce_sum | solution.py:39
  48.4 10.1 %all-reduce = (f32[3072]{0:T(1024)S(1)}, f32[512]{0:T(512)S(1)}) all-reduce(f32[3072]{0:T(1024)S(1)} %bitcast.51, f32[512]{0:T(512)S(1)} %multiply_reduce_fusion.1), channel_id=1, replica_groups=mesh['groups'=2,'seq'=4,'mp'=2,'enc'=2] {'mp','enc'}, use_global_device_ids=true, to_apply=%region_8.9 | all-reduce | flops 3584 | bytes 28672 | tf_op jit(solution)/shard_map/psum | solution.py:39
  58.5 3.5 %all-to-all-start = ((bf16[4,1024,128]{2,1,0:T(8,128)(2,1)}), bf16[4,1024,128]{2,1,0:T(8,128)(2,1)S(1)}, u32[]{:S(2)}, u32[]{:S(2)}) async-start(bf16[4,1024,128]{2,1,0:T(8,128)(2,1)} %bitcast), calls=%async_computation | async-start | bytes 2097152 | tf_op jit(solution)/shard_map/all_to_all | solution.py:35
  62.1 42.8 %reduce-scatter.5.cloned.1.call-done = f32[3072,128]{1,0:T(8,128)} async-done(((f32[3072,512]{1,0:T(8,128)}), f32[3072,128]{1,0:T(8,128)}) %reduce-scatter.5.cloned.1.call-update) | async-done | bytes 1572880 | tf_op jit(solution)/shard_map/reduce_scatter | solution.py:37
  104.8 1.9 %multiply_convert_fusion = bf16[3072,128]{1,0:T(8,128)(2,1)S(1)} fusion(f32[3072,128]{1,0:T(8,128)} %reduce-scatter.5.cloned.1.call-done, f32[3072]{0:T(1024)S(1)} %add_rsqrt_fusion), kind=kLoop, calls=%fused_computation.6 | loop fusion | flops 786432 | bytes 2371584 | tf_op jit(solution)/shard_map/convert_element_type | solution.py:46
  107.1 1.5 fusion.1
  108.6 4.6 %all-to-all-start.3 = ((bf16[4,8,16384]{2,1,0:T(8,128)(2,1)}), bf16[4,8,16384]{2,1,0:T(8,128)(2,1)S(1)}, u32[]{:S(2)}, u32[]{:S(2)}) async-start(bf16[4,8,16384]{2,1,0:T(8,128)(2,1)} %fusion.1), calls=%async_computation.5 | async-start | bytes 2097152 | tf_op jit(solution)/shard_map/all_to_all | solution.py:91
  113.8 3.0 %fusion.32 = f32[512,512]{1,0:T(8,128)} fusion(bf16[512,1024]{1,0:T(8,128)(2,1)} %param.6, bf16[1024,512]{0,1:T(8,128)(2,1)S(1)} %bitcast.43), kind=kOutput, calls=%fused_computation.52 | convolution fusion | flops 536870912 | bytes 3145728 | tf_op jit(solution)/shard_map/dot_general | solution.py:36
  117.3 0.7 reduce.4
  118.1 20.9 %all-to-all-done.3 = bf16[4,8,16384]{2,1,0:T(8,128)(2,1)S(1)} async-done(((bf16[4,8,16384]{2,1,0:T(8,128)(2,1)}), bf16[4,8,16384]{2,1,0:T(8,128)(2,1)S(1)}, u32[]{:S(2)}, u32[]{:S(2)}) %all-to-all-start.3) | async-done | bytes 1048608 | tf_op jit(solution)/shard_map/all_to_all | solution.py:91
  139.4 1.9 %collective-permute-done = bf16[16,128,128]{2,1,0:T(8,128)(2,1)S(1)} collective-permute-done((bf16[16,128,128]{2,1,0:T(8,128)(2,1)S(1)}, bf16[16,128,128]{2,1,0:T(8,128)(2,1)S(1)}, u32[]{:S(2)}, u32[]{:S(2)}) %collective-permute-start) | collective-permute-done | bytes 524320 | tf_op jit(solution)/shard_map/ppermute | solution.py:23
  141.4 1.3 collective-permute-start.1
  142.8 1.1 multiply_convert_fusion.1
  143.9 2.9 %collective-permute-start.2 = (bf16[256,128]{1,0:T(8,128)(2,1)S(1)}, bf16[256,128]{1,0:T(8,128)(2,1)S(1)}, u32[]{:S(2)}, u32[]{:S(2)}) collective-permute-start(bf16[256,128]{1,0:T(8,128)(2,1)S(1)} %bitcast.50), channel_id=1, source_target_pairs={{0,4},{4,8},{8,12},{1,5},{5,9},{9,13},{2,6},{6,10},{10,14},{3,7},{... | collective-permute-start | bytes 196616 | tf_op jit(solution)/shard_map/ppermute | solution.py:29
  147.6 1.1 collective-permute-done.2
  148.7 1.6 %convolution_convert_fusion.2 = bf16[8,64,128]{2,1,0:T(8,128)(2,1)} fusion(bf16[7,256,128]{2,1,0:T(8,128)(2,1)S(1)} %bitcast.46, bf16[1,256,128]{2,1,0:T(8,128)(2,1)S(1)} %bitcast.52, f32[8,64]{1,0:T(8,128)S(1)} %fusion.29, f32[8,64,256]{2,1,0:T(8,128)S(1)} %fusion.6), kind=kOutput, calls=%fused_computation.10 | convolution fusion | flops 34276096 | bytes 1181696 | tf_op jit(solution)/shard_map/cqk,ckd->cqd/dot_general | solution.py:106
  (35 shorter events, 3.5 us)
Async XLA Ops:
  6.5 98.3 %reduce-scatter.5.cloned.1.call-start = ((), (), s32[]{:S(2)}) async-start(), calls=%async_computation.7 | async-start | bytes 7864320 | tf_op jit(solution)/shard_map/reduce_scatter | solution.py:37
  34.0 0.7 copy-start.1
  34.0 1.9 %copy-start.2 = (s32[24]{0:T(128)S(1)}, s32[24]{0:T(128)}, u32[]{:S(2)}) copy-start(s32[24]{0:T(128)} %param.9) | copy-start | bytes 292
  34.0 8.5 %copy-start = (bf16[512,1024]{1,0:T(8,128)(2,1)S(1)}, bf16[512,1024]{1,0:T(8,128)(2,1)}, u32[]{:S(2)}) copy-start(bf16[512,1024]{1,0:T(8,128)(2,1)} %param.6) | copy-start | bytes 3145732
  36.9 21.6 %all-to-all-start.1 = ((s32[4,1,8]{2,1,0:T(1,128)}), s32[4,1,8]{2,1,0:T(1,128)S(1)}, u32[]{:S(2)}, u32[]{:S(2)}) async-start(s32[4,1,8]{2,1,0:T(1,128)} %bitcast.4), calls=%async_computation.2 | async-start | bytes 4096 | tf_op jit(solution)/shard_map/all_to_all | solution.py:92
  58.5 50.1 %all-to-all-start = ((bf16[4,1024,128]{2,1,0:T(8,128)(2,1)}), bf16[4,1024,128]{2,1,0:T(8,128)(2,1)S(1)}, u32[]{:S(2)}, u32[]{:S(2)}) async-start(bf16[4,1024,128]{2,1,0:T(8,128)(2,1)} %bitcast), calls=%async_computation | async-start | bytes 2097152 | tf_op jit(solution)/shard_map/all_to_all | solution.py:35
  108.6 30.3 %all-to-all-start.3 = ((bf16[4,8,16384]{2,1,0:T(8,128)(2,1)}), bf16[4,8,16384]{2,1,0:T(8,128)(2,1)S(1)}, u32[]{:S(2)}, u32[]{:S(2)}) async-start(bf16[4,8,16384]{2,1,0:T(8,128)(2,1)} %fusion.1), calls=%async_computation.5 | async-start | bytes 2097152 | tf_op jit(solution)/shard_map/all_to_all | solution.py:91
  113.2 29.5 %reduce-scatter.3.cloned.1.call-start = ((), (), s32[]{:S(2)}) async-start(), calls=%async_computation.6 | async-start | bytes 1310720 | tf_op jit(solution)/shard_map/reduce_scatter | solution.py:37
  139.3 2.0 %collective-permute-start = (bf16[16,128,128]{2,1,0:T(8,128)(2,1)S(1)}, bf16[16,128,128]{2,1,0:T(8,128)(2,1)S(1)}, u32[]{:S(2)}, u32[]{:S(2)}) collective-permute-start(bf16[16,128,128]{2,1,0:T(8,128)(2,1)S(1)} %bitcast.38), channel_id=1, source_target_pairs={{0,1},{1,0},{2,3},{3,2},{4,5},{5,4},{6,7},{7,6},{8,9},{9,8},{10,11... | collective-permute-start | bytes 1572872 | tf_op jit(solution)/shard_map/ppermute | solution.py:23
  141.4 5.4 %collective-permute-start.1 = (bf16[256,128]{1,0:T(8,128)(2,1)S(1)}, bf16[256,128]{1,0:T(8,128)(2,1)S(1)}, u32[]{:S(2)}, u32[]{:S(2)}) collective-permute-start(bf16[256,128]{1,0:T(8,128)(2,1)S(1)} %bitcast.49), channel_id=1, source_target_pairs={{0,4},{4,8},{8,12},{1,5},{5,9},{9,13},{2,6},{6,10},{10,14},{3,7},{... | collective-permute-start | bytes 196616 | tf_op jit(solution)/shard_map/ppermute | solution.py:29
  143.9 4.8 %collective-permute-start.2 = (bf16[256,128]{1,0:T(8,128)(2,1)S(1)}, bf16[256,128]{1,0:T(8,128)(2,1)S(1)}, u32[]{:S(2)}, u32[]{:S(2)}) collective-permute-start(bf16[256,128]{1,0:T(8,128)(2,1)S(1)} %bitcast.50), channel_id=1, source_target_pairs={{0,4},{4,8},{8,12},{1,5},{5,9},{9,13},{2,6},{6,10},{10,14},{3,7},{... | collective-permute-start | bytes 196616 | tf_op jit(solution)/shard_map/ppermute | solution.py:29
Sparse Core Ops, SparseCore 0:
  34.1 70.6 reduce-scatter.4
  116.9 25.3 reduce-scatter.2
where the time goes:
time: 158 us; the launch traced here: 157 us
  waiting for transfers between devices  66.7 us (42%)
  blocking collectives  28.8 us (18%)
  starting transfers between devices  18 us (11%)
  matrix products  15.4 us (10%)
  between operations  13.6 us (9%)
  other arithmetic  11.2 us (7%)
  local copies, waits for them, and re-layouts  3.44 us (2%)
    reduce_scatter x2, waiting for transfers between devices, project_fold(): lax.psum_scatter(partial, ('mp', 'enc'), scatter_dimension=1, tiled=True)  42.8 us
    all_to_all x1, waiting for transfers between devices, local(): lax.all_to_all(packed, 'seq', split_axis=0, concat_axis=0, tiled=True)  20.9 us
    all_to_all x1, blocking collectives, project_fold(): lax.all_to_all(weight, ('mp', 'enc'), split_axis=0, concat_axis=1, tiled=...  18.7 us
    dot_general x2, matrix products, project_fold(): partial = jnp.dot(flat_rows, mine, preferred_element_type=jnp.float32)  11.3 us
    psum x1, blocking collectives, project_fold(): squares = lax.psum(jnp.sum(widened * widened, axis=1), ('mp', 'enc'))  10.1 us
    reduce_sum x2, other arithmetic, project_fold(): squares = lax.psum(jnp.sum(widened * widened, axis=1), ('mp', 'enc'))  5.83 us
    all_to_all x1, starting transfers between devices, local(): lax.all_to_all(sent_ids, 'seq', split_axis=0, concat_axis=0, tiled=True)  5.6 us
    all_to_all x1, starting transfers between devices, local(): lax.all_to_all(packed, 'seq', split_axis=0, concat_axis=0, tiled=True)  4.63 us
  transfers between devices with their start and end apart: 8, of which 4 were waited for; matrix products, arithmetic and copies ran while one was open for 12% of the time, Pallas kernels for 0%

commit v1 on v0

--- a/solution.py
+++ b/solution.py
@@ -1,7 +1,9 @@
+import functools
 import jax
 import jax.numpy as jnp
 from jax import lax
 from jax.sharding import PartitionSpec as P
+from jax.lax import axis_index, axis_size, ppermute
 
 D = 4096
 SPAN = 64
@@ -11,6 +13,42 @@
 NB_SEQ = 16
 ENC_CAP = 24
 epsilon = 1e-05
+
+
+def chains_update(vec, ndim_at, mine_x):
+    lower = vec.shape
+    kept_arr = vec.reshape(
+        *lower[:ndim_at], mine_x, lower[ndim_at] // mine_x, *lower[ndim_at + 1 :]
+    )
+    t_next = jnp.moveaxis(kept_arr, ndim_at, 0)
+    return t_next
+
+
+def follow_seats_all(mat, dim_at):
+    mat = jnp.moveaxis(mat, 0, dim_at)
+    earlier = mat.shape
+    later = mat.reshape(
+        *earlier[:dim_at], earlier[dim_at] * earlier[dim_at + 1], *earlier[dim_at + 2 :]
+    )
+    return later
+
+
+def stacks_all_form(in_array, a_name, block_in, xin):
+    m_next = axis_size(a_name)
+    r_now = axis_index(a_name)
+    f_now, piece_now = (m_next, r_now)
+    arr_next = chains_update(in_array, block_in, f_now)
+    store = [arr_next[piece_now]]
+    for tick in range(1, f_now):
+        v1 = arr_next[piece_now ^ tick]
+        latest = ppermute(v1, a_name, [(j0, j0 ^ tick) for j0 in range(f_now)])
+        store.append(latest)
+    arr_next = jnp.stack(store)[piece_now ^ jnp.arange(f_now)]
+    big = follow_seats_all(arr_next, xin)
+    return big
+
+
+_time_task = functools.partial(stacks_all_form, a_name="seq", block_in=0, xin=0)
 
 
 def partner_2(block, axis, stride):
@@ -88,7 +126,7 @@
     encoded = normalized(folded, 1.0).reshape(ENC_CAP, RLEN * head_size)
     packed = pack_rows(chosen, encoded, seq_count, pair_cap)
     received, received_ids = (
-        lax.all_to_all(packed, "seq", split_axis=0, concat_axis=0, tiled=True),
+        _time_task(packed),
         lax.all_to_all(sent_ids, "seq", split_axis=0, concat_axis=0, tiled=True),
     )
     own_half = place_rows(received, received_ids).reshape(NB_SEQ, RLEN, head_size)

time: 158 us -> 149 us (0.943)
  waiting for transfers between devices: 66.7 us -> 40.1 us
  blocking collectives: 28.8 us -> 53.3 us
  starting transfers between devices: 18 us -> 12.8 us
    reduce_scatter x2, waiting for transfers between devices: 42.8 us -> 19.3 us  [project_fold(): lax.psum_scatter(partial, ('mp', 'enc'), scatter_dimension=1, tiled=True)]
    all_to_all x2 -> x0, waiting for transfers between devices: 20.9 us -> none  [the longest x1 20.9 us: local(): lax.all_to_all(packed, 'seq', split_axis=0, concat_axis=0, tiled=True)]
    ppermute x0 -> x3, waiting for transfers between devices: none -> 17.8 us  [stacks_all_form(): latest = ppermute(v1, a_name, [(j0, j0 ^ tick) for j0 in range(f_now)])]
    psum x1, blocking collectives: 10.1 us -> 23.7 us  [project_fold(): squares = lax.psum(jnp.sum(widened * widened, axis=1), ('mp', 'enc'))]
    all_to_all x0 -> x1, blocking collectives: none -> 10.9 us  [local(): lax.all_to_all(sent_ids, 'seq', split_axis=0, concat_axis=0, tiled=True)]
    all_to_all x2 -> x0, starting transfers between devices: 10.2 us -> none  [the longest x1 5.6 us: local(): lax.all_to_all(sent_ids, 'seq', split_axis=0, concat_axis=0, tiled=True)]
    ppermute x0 -> x3, starting transfers between devices: none -> 4.45 us  [stacks_all_form(): latest = ppermute(v1, a_name, [(j0, j0 ^ tick) for j0 in range(f_now)])]
  transfers between devices with their start and end apart: 8 -> 9, of which waited for: 4 -> 5; matrix products, arithmetic and copies ran while one was open for 12% -> 10% of each run, Pallas kernels for 0% -> 0%
where the time goes in v1:
time: 149 us; the launch traced here: 148 us
  blocking collectives  53.3 us (36%)
  waiting for transfers between devices  40.1 us (27%)
  matrix products  14.4 us (10%)
  between operations  13.7 us (9%)
  starting transfers between devices  12.8 us (9%)
  other arithmetic  9.83 us (7%)
  local copies, waits for them, and re-layouts  4.4 us (3%)
    psum x1, blocking collectives, project_fold(): squares = lax.psum(jnp.sum(widened * widened, axis=1), ('mp', 'enc'))  23.7 us
    reduce_scatter x2, waiting for transfers between devices, project_fold(): lax.psum_scatter(partial, ('mp', 'enc'), scatter_dimension=1, tiled=True)  19.3 us
    all_to_all x1, blocking collectives, project_fold(): lax.all_to_all(weight, ('mp', 'enc'), split_axis=0, concat_axis=1, tiled=...  18.7 us
    ppermute x3, waiting for transfers between devices, stacks_all_form(): latest = ppermute(v1, a_name, [(j0, j0 ^ tick) for j0 in range(f_now)])  17.8 us
    dot_general x2, matrix products, project_fold(): partial = jnp.dot(flat_rows, mine, preferred_element_type=jnp.float32)  11.2 us
    all_to_all x1, blocking collectives, local(): lax.all_to_all(sent_ids, 'seq', split_axis=0, concat_axis=0, tiled=True)  10.9 us
    ppermute x2, starting transfers between devices, passed_along(): return lax.ppermute(block, axis, route)  4.67 us
    ppermute x3, starting transfers between devices, stacks_all_form(): latest = ppermute(v1, a_name, [(j0, j0 ^ tick) for j0 in range(f_now)])  4.45 us
  transfers between devices with their start and end apart: 9, of which 5 were waited for; matrix products, arithmetic and copies ran while one was open for 10% of the time, Pallas kernels for 0%

profile of v1, /device:TPU:0, one launch (start us, length us, event | category | flops | bytes accessed | tf_op | source)
XLA Modules:
  0.0 148.5 jit_solution(10989234088725827523)
XLA Ops:
  6.5 18.7 %all_to_all.44 = bf16[4,1024,128]{2,1,0:T(8,128)(2,1)S(1)} all-to-all(bf16[4,1024,128]{2,1,0:T(8,128)(2,1)} %bitcast.54), channel_id=1, replica_groups=mesh['groups'=2,'seq'=4,'mp'=2,'enc'=2] {'mp','enc'}, dimensions={0} | all-to-all | bytes 2097152 | tf_op jit(solution)/shard_map/all_to_all | solution.py:73
  25.7 8.2 %fusion.34 = f32[3072,512]{1,0:T(8,128)} fusion(bf16[3072,1024]{1,0:T(8,128)(2,1)} %bitcast.48, bf16[1024,512]{0,1:T(8,128)(2,1)S(1)} %bitcast.56), kind=kOutput, calls=%fused_computation.62 | convolution fusion | flops 3221225472 | bytes 13631488 | tf_op jit(solution)/shard_map/dot_general | solution.py:74
  34.6 0.6 fusion.22
  35.3 0.6 iota_compare_fusion.4
  36.3 10.9 %all_to_all.45 = s32[4,1,8]{2,1,0:T(1,128)S(1)} all-to-all(s32[4,1,8]{2,1,0:T(1,128)S(1)} %bitcast.68), channel_id=1, replica_groups=mesh['groups'=2,'seq'=4,'mp'=2,'enc'=2] {'seq'}, dimensions={0} | all-to-all | bytes 256 | tf_op jit(solution)/shard_map/all_to_all | solution.py:130
  47.3 3.5 %all-to-all-start = ((bf16[4,1024,128]{2,1,0:T(8,128)(2,1)}), bf16[4,1024,128]{2,1,0:T(8,128)(2,1)S(1)}, u32[]{:S(2)}, u32[]{:S(2)}) async-start(bf16[4,1024,128]{2,1,0:T(8,128)(2,1)} %bitcast), calls=%async_computation | async-start | bytes 2097152 | tf_op jit(solution)/shard_map/all_to_all | solution.py:73
  50.9 4.1 %multiply_reduce_fusion = f32[24,128]{1,0:T(8,128)S(1)} fusion(bf16[24,128,1024]{2,1,0:T(8,128)(2,1)} %param.7), kind=kLoop, calls=%fused_computation.5 | loop fusion | flops 9434112 | bytes 6303744 | tf_op jit(solution)/shard_map/reduce_sum | solution.py:77
  55.2 23.7 %all-reduce = (f32[3072]{0:T(1024)S(1)}, f32[512]{0:T(512)S(1)}) all-reduce(f32[3072]{0:T(1024)S(1)} %bitcast.67, f32[512]{0:T(512)S(1)} %multiply_reduce_fusion.1), channel_id=1, replica_groups=mesh['groups'=2,'seq'=4,'mp'=2,'enc'=2] {'mp','enc'}, use_global_device_ids=true, to_apply=%region_8.9 | all-reduce | flops 3584 | bytes 28672 | tf_op jit(solution)/shard_map/psum | solution.py:77
  79.5 0.7 reduce.4
  80.2 1.4 copy.12
  81.6 19.3 %reduce-scatter.5.cloned.1.call-done = f32[3072,128]{1,0:T(8,128)} async-done(((f32[3072,512]{1,0:T(8,128)}), f32[3072,128]{1,0:T(8,128)}) %reduce-scatter.5.cloned.1.call-update) | async-done | bytes 1572880 | tf_op jit(solution)/shard_map/reduce_scatter | solution.py:75
  100.9 1.9 %multiply_convert_fusion = bf16[3072,128]{1,0:T(8,128)(2,1)S(1)} fusion(f32[3072,128]{1,0:T(8,128)} %reduce-scatter.5.cloned.1.call-done, f32[3072]{0:T(1024)S(1)} %add_rsqrt_fusion), kind=kLoop, calls=%fused_computation.7 | loop fusion | flops 786432 | bytes 2371584 | tf_op jit(solution)/shard_map/convert_element_type | solution.py:84
  103.8 0.7 collective-permute-start.2
  104.4 1.5 collective-permute-start.1
  105.9 2.3 %collective-permute-start = (bf16[1,8,16384]{2,1,0:T(8,128)(2,1)S(1)}, bf16[1,8,16384]{2,1,0:T(8,128)(2,1)S(1)}, u32[]{:S(2)}, u32[]{:S(2)}) collective-permute-start(bf16[1,8,16384]{2,1,0:T(8,128)(2,1)S(1)} %get-tuple-element.12), channel_id=1, source_target_pairs={{0,4},{4,0},{8,12},{12,8},{1,5},{5,1},{9,13},{13,9},{2,6},{6,2},{1... | collective-permute-start | bytes 786440 | tf_op jit(solution)/shard_map/ppermute | solution.py:44
  108.2 3.0 %fusion.33 = f32[512,512]{1,0:T(8,128)} fusion(bf16[512,1024]{1,0:T(8,128)(2,1)S(1)} %copy-done, bf16[1024,512]{0,1:T(8,128)(2,1)} %bitcast.55), kind=kOutput, calls=%fused_computation.61 | convolution fusion | flops 536870912 | bytes 3145728 | tf_op jit(solution)/shard_map/dot_general | solution.py:74
  111.2 3.7 %collective-permute-done.2 = bf16[1,8,16384]{2,1,0:T(8,128)(2,1)S(1)} collective-permute-done((bf16[1,8,16384]{2,1,0:T(8,128)(2,1)S(1)}, bf16[1,8,16384]{2,1,0:T(8,128)(2,1)S(1)}, u32[]{:S(2)}, u32[]{:S(2)}) %collective-permute-start.2) | collective-permute-done | bytes 262176 | tf_op jit(solution)/shard_map/ppermute | solution.py:44
  114.9 14.0 %collective-permute-done.1 = bf16[1,8,16384]{2,1,0:T(8,128)(2,1)S(1)} collective-permute-done((bf16[1,8,16384]{2,1,0:T(8,128)(2,1)S(1)}, bf16[1,8,16384]{2,1,0:T(8,128)(2,1)S(1)}, u32[]{:S(2)}, u32[]{:S(2)}) %collective-permute-start.1) | collective-permute-done | bytes 262176 | tf_op jit(solution)/shard_map/ppermute | solution.py:44
  130.2 1.9 %collective-permute-done.3 = bf16[16,128,128]{2,1,0:T(8,128)(2,1)S(1)} collective-permute-done((bf16[16,128,128]{2,1,0:T(8,128)(2,1)S(1)}, bf16[16,128,128]{2,1,0:T(8,128)(2,1)S(1)}, u32[]{:S(2)}, u32[]{:S(2)}) %collective-permute-start.3) | collective-permute-done | bytes 524320 | tf_op jit(solution)/shard_map/ppermute | solution.py:61
  132.2 1.3 collective-permute-start.4
  133.5 1.1 multiply_convert_fusion.1
  134.7 3.4 %collective-permute-start.5 = (bf16[256,128]{1,0:T(8,128)(2,1)S(1)}, bf16[256,128]{1,0:T(8,128)(2,1)S(1)}, u32[]{:S(2)}, u32[]{:S(2)}) collective-permute-start(bf16[256,128]{1,0:T(8,128)(2,1)S(1)} %bitcast.66), channel_id=1, source_target_pairs={{0,4},{4,8},{8,12},{1,5},{5,9},{9,13},{2,6},{6,10},{10,14},{3,7},{... | collective-permute-start | bytes 196616 | tf_op jit(solution)/shard_map/ppermute | solution.py:67
  138.9 1.1 collective-permute-done.5
  140.0 1.6 %convolution_convert_fusion.2 = bf16[8,64,128]{2,1,0:T(8,128)(2,1)} fusion(bf16[7,256,128]{2,1,0:T(8,128)(2,1)S(1)} %bitcast.59, bf16[1,256,128]{2,1,0:T(8,128)(2,1)S(1)} %bitcast.69, f32[8,64]{1,0:T(8,128)S(1)} %fusion.30, f32[8,64,256]{2,1,0:T(8,128)S(1)} %fusion.6), kind=kOutput, calls=%fused_computation.11 | convolution fusion | flops 34276096 | bytes 1181696 | tf_op jit(solution)/shard_map/cqk,ckd->cqd/dot_general | solution.py:144
  (43 shorter events, 5.6 us)
Async XLA Ops:
  6.5 94.4 %reduce-scatter.5.cloned.1.call-start = ((), (), s32[]{:S(2)}) async-start(), calls=%async_computation.6 | async-start | bytes 7864320 | tf_op jit(solution)/shard_map/reduce_scatter | solution.py:75
  34.0 0.7 copy-start.1
  34.0 1.9 %copy-start.2 = (s32[24]{0:T(128)S(1)}, s32[24]{0:T(128)}, u32[]{:S(2)}) copy-start(s32[24]{0:T(128)} %param.9) | copy-start | bytes 292
  34.0 21.0 %copy-start = (bf16[512,1024]{1,0:T(8,128)(2,1)S(1)}, bf16[512,1024]{1,0:T(8,128)(2,1)}, u32[]{:S(2)}) copy-start(bf16[512,1024]{1,0:T(8,128)(2,1)} %param.6) | copy-start | bytes 3145732
  47.3 33.0 %all-to-all-start = ((bf16[4,1024,128]{2,1,0:T(8,128)(2,1)}), bf16[4,1024,128]{2,1,0:T(8,128)(2,1)S(1)}, u32[]{:S(2)}, u32[]{:S(2)}) async-start(bf16[4,1024,128]{2,1,0:T(8,128)(2,1)} %bitcast), calls=%async_computation | async-start | bytes 2097152 | tf_op jit(solution)/shard_map/all_to_all | solution.py:73
  50.8 82.7 %reduce-scatter.3.cloned.1.call-start = ((), (), s32[]{:S(2)}) async-start(), calls=%async_computation.5 | async-start | bytes 1310720 | tf_op jit(solution)/shard_map/reduce_scatter | solution.py:75
  103.8 11.2 %collective-permute-start.2 = (bf16[1,8,16384]{2,1,0:T(8,128)(2,1)S(1)}, bf16[1,8,16384]{2,1,0:T(8,128)(2,1)S(1)}, u32[]{:S(2)}, u32[]{:S(2)}) collective-permute-start(bf16[1,8,16384]{2,1,0:T(8,128)(2,1)S(1)} %get-tuple-element.10), channel_id=1, source_target_pairs={{0,12},{4,8},{8,4},{12,0},{1,13},{5,9},{9,5},{13,1},{2,14},{6,10},... | collective-permute-start | bytes 786440 | tf_op jit(solution)/shard_map/ppermute | solution.py:44
  104.4 24.6 %collective-permute-start.1 = (bf16[1,8,16384]{2,1,0:T(8,128)(2,1)S(1)}, bf16[1,8,16384]{2,1,0:T(8,128)(2,1)S(1)}, u32[]{:S(2)}, u32[]{:S(2)}) collective-permute-start(bf16[1,8,16384]{2,1,0:T(8,128)(2,1)S(1)} %get-tuple-element.11), channel_id=1, source_target_pairs={{0,8},{4,12},{8,0},{12,4},{1,9},{5,13},{9,1},{13,5},{2,10},{6,14},... | collective-permute-start | bytes 786440 | tf_op jit(solution)/shard_map/ppermute | solution.py:44
  105.9 23.1 %collective-permute-start = (bf16[1,8,16384]{2,1,0:T(8,128)(2,1)S(1)}, bf16[1,8,16384]{2,1,0:T(8,128)(2,1)S(1)}, u32[]{:S(2)}, u32[]{:S(2)}) collective-permute-start(bf16[1,8,16384]{2,1,0:T(8,128)(2,1)S(1)} %get-tuple-element.12), channel_id=1, source_target_pairs={{0,4},{4,0},{8,12},{12,8},{1,5},{5,1},{9,13},{13,9},{2,6},{6,2},{1... | collective-permute-start | bytes 786440 | tf_op jit(solution)/shard_map/ppermute | solution.py:44
  130.1 2.0 %collective-permute-start.3 = (bf16[16,128,128]{2,1,0:T(8,128)(2,1)S(1)}, bf16[16,128,128]{2,1,0:T(8,128)(2,1)S(1)}, u32[]{:S(2)}, u32[]{:S(2)}) collective-permute-start(bf16[16,128,128]{2,1,0:T(8,128)(2,1)S(1)} %bitcast.51), channel_id=1, source_target_pairs={{0,1},{1,0},{2,3},{3,2},{4,5},{5,4},{6,7},{7,6},{8,9},{9,8},{10,11... | collective-permute-start | bytes 1572872 | tf_op jit(solution)/shard_map/ppermute | solution.py:61
  132.2 5.9 %collective-permute-start.4 = (bf16[256,128]{1,0:T(8,128)(2,1)S(1)}, bf16[256,128]{1,0:T(8,128)(2,1)S(1)}, u32[]{:S(2)}, u32[]{:S(2)}) collective-permute-start(bf16[256,128]{1,0:T(8,128)(2,1)S(1)} %bitcast.65), channel_id=1, source_target_pairs={{0,4},{4,8},{8,12},{1,5},{5,9},{9,13},{2,6},{6,10},{10,14},{3,7},{... | collective-permute-start | bytes 196616 | tf_op jit(solution)/shard_map/ppermute | solution.py:67
  134.7 5.3 %collective-permute-start.5 = (bf16[256,128]{1,0:T(8,128)(2,1)S(1)}, bf16[256,128]{1,0:T(8,128)(2,1)S(1)}, u32[]{:S(2)}, u32[]{:S(2)}) collective-permute-start(bf16[256,128]{1,0:T(8,128)(2,1)S(1)} %bitcast.66), channel_id=1, source_target_pairs={{0,4},{4,8},{8,12},{1,5},{5,9},{9,13},{2,6},{6,10},{10,14},{3,7},{... | collective-permute-start | bytes 196616 | tf_op jit(solution)/shard_map/ppermute | solution.py:67
Sparse Core Ops, SparseCore 0:
  34.1 66.7 reduce-scatter.4
  111.3 22.1 reduce-scatter.2
